TPU v7x, 128 devices: a whole 4x4x4 slice. The times are simulated.
128 devices in a mesh: row: 8 (over z, x_hi), col: 16 (over x_lo, y, core).
Axes of the slice: x: 4 (x_hi: 2, x_lo: 2; x = x_hi * 2 + x_lo), y: 4, z: 4, core: 2. Of those that a mesh axis runs over, the one named last changes fastest.
Arguments:
- ingest_features: bfloat16 [32768, 1536], P(('row', 'col')), may hold values from -40 to 40
- node_map: int32 [32768], P(('row', 'col')), may hold values from 0 to 16383, as said below
- unit_rows: int32 [128], P(('row', 'col')), may hold values from 0 to 256, as said below
- tile_ids: int32 [12288, 2], P(('row', 'col')), may hold values from 0 to 128, as said below
- tile_values: bfloat16 [12288, 128, 128], P(('row', 'col')), may hold values from -40 to 40
- mix_in: bfloat16 [128, 128], replicated, may hold values from -0.5 to 0.5
- mix_out: bfloat16 [128, 128], replicated, may hold values from -0.5 to 0.5
Outputs:
- residual: float32 [16384, 1536], P(('row', 'col'))
Inputs may be any that keep to these rules, and one draw needn't show every extreme that they name: `node_map`: for every unit u the first unit_rows[u] of its 256 slots name distinct nodes, and all units' such slots together name every node exactly once; at most 2 of them of one unit name nodes of one partition (nodes k * 128 to (k + 1) * 128 - 1), and one unit names exactly 2 in every partition. Entries of the other slots are arbitrary nodes. `unit_rows`: one unit delivers 256 rows. `tile_ids`: slots k * 96 to (k + 1) * 96 - 1 hold first some distinct tiles whose row tile lies in row block k // 16 (tile rows (16 times that) onward) and whose column tile lies in column block k % 16, then padding slots whose row tile and column tile are both 16384 // 128. Some blocks have no padding slot.
All inputs are finite; a program needn't handle non-finite values.
Results may differ from a plain program's by a relative error of at most 0.0095.
Values may be sent and summed in bfloat16 or wider, within the bound.
A program may use at most 64 MiB of HBM per device.

v0:
```python
import jax
import jax.numpy as jnp
from jax import lax
from jax.sharding import PartitionSpec as P

CH = 128
TILE = 128
PIECE = 128
epsilon = 1e-05


def normalize(values):
    groups = values.reshape(-1, CH)
    power = jnp.mean(groups * groups, axis=-1, keepdims=True)
    return (groups * lax.rsqrt(power + epsilon)).astype(jnp.bfloat16)


def encode(totals, mix_in):
    row_total = totals.shape[0]
    mixed = jnp.dot(normalize(totals), mix_in, preferred_element_type=jnp.float32)
    return jax.nn.gelu(mixed, approximate=False).astype(jnp.bfloat16).reshape(row_total, -1)


def dense_block(tile_ids, tile_values, row_index, col_index, row_tiles, col_tiles):
    local_rows = tile_ids[:, 0] - row_index * row_tiles
    local_cols = tile_ids[:, 1] - col_index * col_tiles
    tile_edge = tile_values.shape[1]
    tile_grid = jnp.zeros((row_tiles, col_tiles, tile_edge, tile_edge), tile_values.dtype)
    tile_grid = tile_grid.at[local_rows, local_cols].set(tile_values, mode="drop")
    return tile_grid.transpose(0, 2, 1, 3).reshape(row_tiles * tile_edge, col_tiles * tile_edge)


def local(ingest_features, node_map, unit_rows, tile_ids, tile_values, mix_in, mix_out):
    row_count = lax.axis_size("row")
    col_count = lax.axis_size("col")
    unit_count = row_count * col_count
    slots_held = node_map.shape[0]
    per_pair = slots_held // unit_count
    feature_width = ingest_features.shape[1]
    owner = node_map // PIECE
    live = jnp.arange(slots_held, dtype=jnp.int32) < unit_rows[0]
    member = (
        (owner[:, None] == jnp.arange(unit_count, dtype=jnp.int32)[None, :]) & live[:, None]
    ).astype(jnp.int32)
    earlier = jnp.cumsum(member, axis=0) - member
    rank_within = jnp.sum(earlier * member, axis=1)
    target = jnp.where(live, owner * per_pair + rank_within, unit_count * per_pair)
    outgoing = (
        jnp.zeros((unit_count * per_pair, feature_width), jnp.bfloat16)
        .at[target]
        .set(ingest_features, mode="drop")
    )
    placing = (
        jnp.full((unit_count * per_pair,), -1, jnp.int32)
        .at[target]
        .set(node_map % PIECE, mode="drop")
    )
    arrived, arrived_at = (
        lax.all_to_all(
            outgoing.reshape(unit_count, per_pair, feature_width),
            ("row", "col"),
            split_axis=0,
            concat_axis=0,
            tiled=True,
        ),
        lax.all_to_all(
            placing.reshape(unit_count, per_pair),
            ("row", "col"),
            split_axis=0,
            concat_axis=0,
            tiled=True,
        ),
    )
    arrived = arrived.reshape(-1, feature_width)
    arrived_at = arrived_at.reshape(-1)
    landing = jnp.where(arrived_at >= 0, arrived_at, PIECE)
    features = jnp.zeros((PIECE, feature_width), jnp.bfloat16).at[landing].set(arrived, mode="drop")
    row_tiles = col_count * PIECE // TILE
    col_tiles = row_count * PIECE // TILE
    block = dense_block(
        tile_ids, tile_values, lax.axis_index("row"), lax.axis_index("col"), row_tiles, col_tiles
    )
    strip = block
    back_part = lax.dot_general(
        strip,
        lax.all_gather(features, "col", axis=0, tiled=True),
        (((0,), (0,)), ((), ())),
        preferred_element_type=jnp.float32,
    )
    back_own = lax.psum_scatter(
        back_part.astype(jnp.bfloat16), "row", scatter_dimension=0, tiled=True
    ).astype(jnp.float32)
    hidden = lax.all_gather(encode(back_own, mix_in), "row", axis=0, tiled=True)
    strip = block
    forward_sum = lax.psum_scatter(
        jnp.dot(strip, hidden, preferred_element_type=jnp.float32).astype(jnp.bfloat16),
        "col",
        scatter_dimension=0,
        tiled=True,
    ).astype(jnp.float32)
    recon = jnp.dot(normalize(forward_sum), mix_out, preferred_element_type=jnp.float32).reshape(
        PIECE, feature_width
    )
    return features.astype(jnp.float32) - recon


def solution(mesh):
    return jax.shard_map(
        local,
        mesh=mesh,
        in_specs=(
            P(("row", "col"), None),
            P(("row", "col")),
            P(("row", "col")),
            P(("row", "col"), None),
            P(("row", "col"), None, None),
            P(),
            P(),
        ),
        out_specs=P(("row", "col"), None),
        check_vma=False,
    )
```

profile of v0, /device:TPU:0, one launch (start us, length us, event | category | flops | bytes accessed | tf_op | source)
XLA Modules:
  0.0 343.9 jit_solution(6542489902503923748)
XLA Ops:
  8.7 1.4 scatter_custom_fusion
  10.9 11.1 %all-to-all-start = ((s32[128,1,2]{2,1,0:T(1,128)}), s32[128,1,2]{2,1,0:T(1,128)S(1)}, u32[]{:S(2)}, u32[]{:S(2)}) async-start(s32[128,1,2]{2,1,0:T(1,128)} %bitcast.5), calls=%async_computation | async-start | bytes 131072 | tf_op jit(solution)/shard_map/all_to_all | solution.py:66
  22.0 2.6 scatter_custom_fusion.1
  24.6 1.2 reshape.107
  25.8 5.5 %all-to-all-done = s32[128,1,2]{2,1,0:T(1,128)S(1)} async-done(((s32[128,1,2]{2,1,0:T(1,128)}), s32[128,1,2]{2,1,0:T(1,128)S(1)}, u32[]{:S(2)}, u32[]{:S(2)}) %all-to-all-start) | async-done | bytes 1056 | tf_op jit(solution)/shard_map/all_to_all | solution.py:66
  31.3 4.7 %all-to-all-start.1 = ((bf16[128,2,1536]{2,1,0:T(2,128)(2,1)}), bf16[128,2,1536]{2,1,0:T(2,128)(2,1)S(1)}, u32[]{:S(2)}, u32[]{:S(2)}) async-start(bf16[128,2,1536]{2,1,0:T(2,128)(2,1)} %reshape.107), calls=%async_computation.1 | async-start | bytes 1572864 | tf_op jit(solution)/shard_map/all_to_all | solution.py:59
  36.7 0.8 reduce.3
  37.7 14.6 %all-to-all-done.1 = bf16[128,2,1536]{2,1,0:T(2,128)(2,1)S(1)} async-done(((bf16[128,2,1536]{2,1,0:T(2,128)(2,1)}), bf16[128,2,1536]{2,1,0:T(2,128)(2,1)S(1)}, u32[]{:S(2)}, u32[]{:S(2)}) %all-to-all-start.1) | async-done | bytes 786464 | tf_op jit(solution)/shard_map/all_to_all | solution.py:59
  52.3 1.2 reshape.140
  53.5 3.2 scatter_custom_fusion.2
  57.0 3.1 broadcast_in_dim.34
  60.2 13.7 %scatter_fusion = bf16[16,8,128,128]{3,2,1,0:T(8,128)(2,1)} fusion(bf16[16,8,128,128]{3,2,1,0:T(8,128)(2,1)} %broadcast_in_dim.34, s32[96]{0:T(128)S(1)} %fusion.36, bf16[96,128,128]{2,1,0:T(8,128)(2,1)S(1)} %copy-done.2), kind=kCustom, calls=%fused_computation.3 | custom fusion | bytes 9437952 | tf_op jit(solution)/shard_map/scatter | solution.py:29
  73.9 7.8 %copy.14 = bf16[16,128,8,128]{3,2,1,0:T(8,128)(2,1)} copy(bf16[16,128,8,128]{3,1,2,0:T(8,128)(2,1)} %bitcast.40) | data formatting | bytes 8388608 | tf_op jit(solution)/shard_map/transpose | solution.py:30
  81.7 13.3 %all-gather.3.cloned.1.call-done = bf16[2048,1536]{1,0:T(8,128)(2,1)} async-done(((bf16[128,1536]{1,0:T(8,128)(2,1)}), bf16[2048,1536]{1,0:T(8,128)(2,1)}) %all-gather.3.cloned.1.call-update) | async-done | bytes 6291472 | tf_op jit(solution)/shard_map/all_gather | solution.py:86
  95.0 11.4 %fusion.3 = bf16[1024,1536]{1,0:T(8,128)(2,1)} fusion(bf16[2048,1536]{1,0:T(8,128)(2,1)} %all-gather.3.cloned.1.call-done, bf16[256,8,8,128]{3,2,1,0:T(8,128)(2,1)} %bitcast.41), kind=kOutput, calls=%fused_computation.8 | convolution fusion | flops 6444023808 | bytes 13631488 | tf_op jit(solution)/shard_map/dot_general | solution.py:84
  106.5 80.5 %reduce-scatter.3.cloned.1.call-done = bf16[128,1536]{1,0:T(8,128)(2,1)} async-done(((bf16[1024,1536]{1,0:T(8,128)(2,1)}), bf16[128,1536]{1,0:T(8,128)(2,1)}) %reduce-scatter.3.cloned.1.call-update) | async-done | bytes 393232 | tf_op jit(solution)/shard_map/reduce_scatter | solution.py:90
  187.0 1.4 reshape.117
  188.7 2.4 fusion.10
  191.1 1.2 reshape.112
  192.6 61.5 %all-gather.5.cloned.1.call-done = bf16[1024,1536]{1,0:T(8,128)(2,1)} async-done(((bf16[128,1536]{1,0:T(8,128)(2,1)}), bf16[1024,1536]{1,0:T(8,128)(2,1)}) %all-gather.5.cloned.1.call-update) | async-done | bytes 3145744 | tf_op jit(solution)/shard_map/all_gather | solution.py:93
  254.1 11.3 %convolution_convert_fusion = bf16[2048,1536]{1,0:T(8,128)(2,1)} fusion(bf16[1024,1536]{1,0:T(8,128)(2,1)} %all-gather.5.cloned.1.call-done, bf16[256,8,8,128]{3,2,1,0:T(8,128)(2,1)} %bitcast.42), kind=kOutput, calls=%fused_computation.4 | convolution fusion | flops 6445596672 | bytes 13631488 | tf_op jit(solution)/shard_map/dot_general | solution.py:96
  265.5 68.6 %reduce-scatter.5.cloned.1.call-done = bf16[128,1536]{1,0:T(8,128)(2,1)} async-done(((bf16[2048,1536]{1,0:T(8,128)(2,1)}), bf16[128,1536]{1,0:T(8,128)(2,1)}) %reduce-scatter.5.cloned.1.call-update) | async-done | bytes 393232 | tf_op jit(solution)/shard_map/reduce_scatter | solution.py:95
  334.1 1.4 reshape.119
  336.4 1.0 convert_subtract_fusion
  (42 shorter events, 4.7 us)
Async XLA Ops:
  6.5 182.2 %copy-start = (bf16[128,128]{1,0:T(8,128)(2,1)S(1)}, bf16[128,128]{1,0:T(8,128)(2,1)}, u32[]{:S(2)}) copy-start(bf16[128,128]{1,0:T(8,128)(2,1)} %param.12) | copy-start | bytes 98308
  6.5 50.5 %copy-start.4 = (s32[96,2]{0,1:T(2,128)S(1)}, s32[96,2]{0,1:T(2,128)}, u32[]{:S(2)}) copy-start(s32[96,2]{0,1:T(2,128)} %param.10) | copy-start | bytes 2308
  10.9 20.5 %all-to-all-start = ((s32[128,1,2]{2,1,0:T(1,128)}), s32[128,1,2]{2,1,0:T(1,128)S(1)}, u32[]{:S(2)}, u32[]{:S(2)}) async-start(s32[128,1,2]{2,1,0:T(1,128)} %bitcast.5), calls=%async_computation | async-start | bytes 131072 | tf_op jit(solution)/shard_map/all_to_all | solution.py:66
  31.3 21.0 %all-to-all-start.1 = ((bf16[128,2,1536]{2,1,0:T(2,128)(2,1)}), bf16[128,2,1536]{2,1,0:T(2,128)(2,1)S(1)}, u32[]{:S(2)}, u32[]{:S(2)}) async-start(bf16[128,2,1536]{2,1,0:T(2,128)(2,1)} %reshape.107), calls=%async_computation.1 | async-start | bytes 1572864 | tf_op jit(solution)/shard_map/all_to_all | solution.py:59
  36.0 59.0 %all-gather.3.cloned.1.call-start = ((), (), s32[]{:S(2)}) async-start(), calls=%async_computation.4 | async-start | bytes 6684672 | tf_op jit(solution)/shard_map/all_gather | solution.py:86
  53.5 6.7 %copy-start.2 = (bf16[96,128,128]{2,1,0:T(8,128)(2,1)S(1)}, bf16[96,128,128]{2,1,0:T(8,128)(2,1)}, u32[]{:S(2)}) copy-start(bf16[96,128,128]{2,1,0:T(8,128)(2,1)} %param.11) | copy-start | bytes 9437188
  56.8 130.2 %reduce-scatter.3.cloned.1.call-start = ((), (), s32[]{:S(2)}) async-start(), calls=%async_computation.5 | async-start | bytes 3538944 | tf_op jit(solution)/shard_map/reduce_scatter | solution.py:90
  106.5 147.7 %all-gather.5.cloned.1.call-start = ((), (), s32[]{:S(2)}) async-start(), calls=%async_computation.6 | async-start | bytes 3538944 | tf_op jit(solution)/shard_map/all_gather | solution.py:93
  192.3 141.7 %reduce-scatter.5.cloned.1.call-start = ((), (), s32[]{:S(2)}) async-start(), calls=%async_computation.7 | async-start | bytes 6684672 | tf_op jit(solution)/shard_map/reduce_scatter | solution.py:95
  265.4 70.4 %copy-start.3 = (bf16[128,128]{1,0:T(8,128)(2,1)S(1)}, bf16[128,128]{1,0:T(8,128)(2,1)}, u32[]{:S(2)}) copy-start(bf16[128,128]{1,0:T(8,128)(2,1)} %param.13) | copy-start | bytes 98308
  265.4 70.9 %copy-start.1 = (bf16[128,1536]{1,0:T(8,128)(2,1)S(1)}, bf16[128,1536]{1,0:T(8,128)(2,1)}, u32[]{:S(2)}) copy-start(bf16[128,1536]{1,0:T(8,128)(2,1)} %scatter_custom_fusion.2) | copy-start | bytes 1179652
Sparse Core Ops, SparseCore 0:
  56.9 38.0 all-gather.2
  106.6 80.3 reduce-scatter.2
  192.5 61.6 all-gather.4
  265.6 68.4 reduce-scatter.4
where the time goes:
time: 345 us; the launch traced here: 344 us
  waiting for transfers between devices  244 us (71%)
  local copies, waits for them, and re-layouts  40.1 us (12%)
  matrix products  25.5 us (7%)
  starting transfers between devices  16.4 us (5%)
  between operations  14 us (4%)
  other arithmetic  3.71 us (1%)
    reduce_scatter x1, waiting for transfers between devices, local(): lax.psum_scatter(back_part.astype(jnp.bfloat16), 'row', scatter_dimension...  80.5 us
    reduce_scatter x1, waiting for transfers between devices, local(): lax.psum_scatter(jnp.dot(strip, hidden, preferred_element_type=jnp.float3...  68.6 us
    all_gather x1, waiting for transfers between devices, local(): hidden = lax.all_gather(encode(back_own, mix_in), 'row', axis=0, tiled=True)  61.5 us
    all_to_all x1, waiting for transfers between devices, local(): lax.all_to_all(outgoing.reshape(unit_count, per_pair, feature_width), ('r...  14.6 us
    scatter x1, local copies, waits for them, and re-layouts, dense_block(): tile_grid.at[local_rows, local_cols].set(tile_values, mode='drop')  13.7 us
    all_gather x1, waiting for transfers between devices, local(): lax.all_gather(features, 'col', axis=0, tiled=True)  13.3 us
    dot_general x1, matrix products, local(): lax.dot_general(strip, lax.all_gather(features, 'col', axis=0, tiled=True...  11.4 us
    dot_general x1, matrix products, local(): jnp.dot(strip, hidden, preferred_element_type=jnp.float32)  11.3 us
  transfers between devices with their start and end apart: 6, of which 6 were waited for; matrix products, arithmetic and copies ran while one was open for 9% of the time, Pallas kernels for 0%

commit v1 on v0

--- a/solution.py
+++ b/solution.py
@@ -83,7 +83,9 @@
     strip = block
     back_part = lax.dot_general(
         strip,
-        lax.all_gather(features, "col", axis=0, tiled=True),
+        jnp.concatenate(
+            lax.all_to_all(jnp.stack([features] * lax.axis_size("col")), "col", 0, 0), axis=0
+        ),
         (((0,), (0,)), ((), ())),
         preferred_element_type=jnp.float32,
     )

time: 345 us -> 403 us (1.17)
  waiting for transfers between devices: 244 us -> 295 us
  starting transfers between devices: 16.4 us -> 21.1 us
    all_to_all x0 -> x1, waiting for transfers between devices: none -> 61.3 us  [local(): lax.all_to_all(jnp.stack([features] * lax.axis_size('col')), 'col', 0, 0)]
    all_gather x1 -> x0, waiting for transfers between devices: 13.3 us -> none  [local(): lax.all_gather(features, 'col', axis=0, tiled=True)]
    all_to_all x0 -> x1, starting transfers between devices: none -> 4.76 us  [local(): lax.all_to_all(jnp.stack([features] * lax.axis_size('col')), 'col', 0, 0)]
  transfers between devices with their start and end apart: 6 -> 6, of which waited for: 6 -> 6; matrix products, arithmetic and copies ran while one was open for 9% -> 8% of each run, Pallas kernels for 0% -> 0%
where the time goes in v1:
time: 403 us; the launch traced here: 402 us
  waiting for transfers between devices  295 us (73%)
  local copies, waits for them, and re-layouts  42.8 us (11%)
  matrix products  25.6 us (6%)
  starting transfers between devices  21.1 us (5%)
  between operations  14 us (3%)
    reduce_scatter x1, waiting for transfers between devices, local(): lax.psum_scatter(back_part.astype(jnp.bfloat16), 'row', scatter_dimension...  83.2 us
    reduce_scatter x1, waiting for transfers between devices, local(): lax.psum_scatter(jnp.dot(strip, hidden, preferred_element_type=jnp.float3...  68.6 us
    all_gather x1, waiting for transfers between devices, local(): hidden = lax.all_gather(encode(back_own, mix_in), 'row', axis=0, tiled=True)  61.5 us
    all_to_all x1, waiting for transfers between devices, local(): lax.all_to_all(jnp.stack([features] * lax.axis_size('col')), 'col', 0, 0)  61.3 us
    scatter x1, local copies, waits for them, and re-layouts, dense_block(): tile_grid.at[local_rows, local_cols].set(tile_values, mode='drop')  15.7 us
    all_to_all x1, waiting for transfers between devices, local(): lax.all_to_all(outgoing.reshape(unit_count, per_pair, feature_width), ('r...  14.7 us
    dot_general x1, matrix products, local(): lax.dot_general(strip, jnp.concatenate(lax.all_to_all(jnp.stack([features...  11.5 us
    dot_general x1, matrix products, local(): jnp.dot(strip, hidden, preferred_element_type=jnp.float32)  11.3 us
  transfers between devices with their start and end apart: 6, of which 6 were waited for; matrix products, arithmetic and copies ran while one was open for 8% of the time, Pallas kernels for 0%

profile of v1, /device:TPU:0, one launch (start us, length us, event | category | flops | bytes accessed | tf_op | source)
XLA Modules:
  0.0 402.1 jit_solution(14900453024285488252)
XLA Ops:
  8.7 1.4 scatter_custom_fusion
  10.9 11.1 %all-to-all-start = ((s32[128,1,2]{2,1,0:T(1,128)}), s32[128,1,2]{2,1,0:T(1,128)S(1)}, u32[]{:S(2)}, u32[]{:S(2)}) async-start(s32[128,1,2]{2,1,0:T(1,128)} %bitcast.5), calls=%async_computation | async-start | bytes 131072 | tf_op jit(solution)/shard_map/all_to_all | solution.py:66
  22.0 2.6 scatter_custom_fusion.1
  24.6 1.2 reshape.112
  25.8 5.5 %all-to-all-done = s32[128,1,2]{2,1,0:T(1,128)S(1)} async-done(((s32[128,1,2]{2,1,0:T(1,128)}), s32[128,1,2]{2,1,0:T(1,128)S(1)}, u32[]{:S(2)}, u32[]{:S(2)}) %all-to-all-start) | async-done | bytes 1056 | tf_op jit(solution)/shard_map/all_to_all | solution.py:66
  31.3 4.7 %all-to-all-start.1 = ((bf16[128,2,1536]{2,1,0:T(2,128)(2,1)}), bf16[128,2,1536]{2,1,0:T(2,128)(2,1)S(1)}, u32[]{:S(2)}, u32[]{:S(2)}) async-start(bf16[128,2,1536]{2,1,0:T(2,128)(2,1)} %reshape.112), calls=%async_computation.1 | async-start | bytes 1572864 | tf_op jit(solution)/shard_map/all_to_all | solution.py:59
  37.6 14.7 %all-to-all-done.1 = bf16[128,2,1536]{2,1,0:T(2,128)(2,1)S(1)} async-done(((bf16[128,2,1536]{2,1,0:T(2,128)(2,1)}), bf16[128,2,1536]{2,1,0:T(2,128)(2,1)S(1)}, u32[]{:S(2)}, u32[]{:S(2)}) %all-to-all-start.1) | async-done | bytes 786464 | tf_op jit(solution)/shard_map/all_to_all | solution.py:59
  52.6 1.9 scatter_custom_fusion.2
  54.5 3.3 stack.2
  57.7 4.8 %all-to-all-start.2 = ((bf16[16,128,1536]{2,1,0:T(8,128)(2,1)}), bf16[16,128,1536]{2,1,0:T(8,128)(2,1)}, u32[]{:S(2)}, u32[]{:S(2)}) async-start(bf16[16,128,1536]{2,1,0:T(8,128)(2,1)} %stack.2), calls=%async_computation.2 | async-start | bytes 12582912 | tf_op jit(solution)/shard_map/all_to_all | solution.py:87
  62.8 3.0 broadcast_in_dim.34
  65.7 15.7 %scatter_fusion = bf16[16,8,128,128]{3,2,1,0:T(8,128)(2,1)} fusion(bf16[16,8,128,128]{3,2,1,0:T(8,128)(2,1)} %broadcast_in_dim.34, s32[96]{0:T(128)S(1)} %fusion.36, bf16[96,128,128]{2,1,0:T(8,128)(2,1)} %param.11), kind=kCustom, calls=%fused_computation.3 | custom fusion | bytes 9437952 | tf_op jit(solution)/shard_map/scatter | solution.py:29
  81.4 7.7 %copy.14 = bf16[16,128,8,128]{3,2,1,0:T(8,128)(2,1)} copy(bf16[16,128,8,128]{3,1,2,0:T(8,128)(2,1)} %bitcast.37) | data formatting | bytes 8388608 | tf_op jit(solution)/shard_map/transpose | solution.py:30
  89.1 61.3 %all-to-all-done.2 = bf16[16,128,1536]{2,1,0:T(8,128)(2,1)} async-done(((bf16[16,128,1536]{2,1,0:T(8,128)(2,1)}), bf16[16,128,1536]{2,1,0:T(8,128)(2,1)}, u32[]{:S(2)}, u32[]{:S(2)}) %all-to-all-start.2) | async-done | bytes 6291488 | tf_op jit(solution)/shard_map/all_to_all | solution.py:87
  150.5 11.5 %fusion.3 = bf16[1024,1536]{1,0:T(8,128)(2,1)} fusion(bf16[2048,1536]{1,0:T(8,128)(2,1)} %bitcast.9, bf16[256,8,8,128]{3,2,1,0:T(8,128)(2,1)} %bitcast.38), kind=kOutput, calls=%fused_computation.8 | convolution fusion | flops 6444023808 | bytes 13631488 | tf_op jit(solution)/shard_map/dot_general | solution.py:84
  162.0 83.2 %reduce-scatter.3.cloned.1.call-done = bf16[128,1536]{1,0:T(8,128)(2,1)} async-done(((bf16[1024,1536]{1,0:T(8,128)(2,1)}), bf16[128,1536]{1,0:T(8,128)(2,1)}) %reduce-scatter.3.cloned.1.call-update) | async-done | bytes 393232 | tf_op jit(solution)/shard_map/reduce_scatter | solution.py:92
  245.2 1.4 reshape.123
  247.0 2.4 fusion.10
  249.4 1.2 reshape.118
  250.9 61.5 %all-gather.2.cloned.1.call-done = bf16[1024,1536]{1,0:T(8,128)(2,1)} async-done(((bf16[128,1536]{1,0:T(8,128)(2,1)}), bf16[1024,1536]{1,0:T(8,128)(2,1)}) %all-gather.2.cloned.1.call-update) | async-done | bytes 3145744 | tf_op jit(solution)/shard_map/all_gather | solution.py:95
  312.4 11.3 %convolution_convert_fusion = bf16[2048,1536]{1,0:T(8,128)(2,1)} fusion(bf16[1024,1536]{1,0:T(8,128)(2,1)} %all-gather.2.cloned.1.call-done, bf16[256,8,8,128]{3,2,1,0:T(8,128)(2,1)} %bitcast.39), kind=kOutput, calls=%fused_computation.4 | convolution fusion | flops 6445596672 | bytes 13631488 | tf_op jit(solution)/shard_map/dot_general | solution.py:98
  323.7 68.6 %reduce-scatter.5.cloned.1.call-done = bf16[128,1536]{1,0:T(8,128)(2,1)} async-done(((bf16[2048,1536]{1,0:T(8,128)(2,1)}), bf16[128,1536]{1,0:T(8,128)(2,1)}) %reduce-scatter.5.cloned.1.call-update) | async-done | bytes 393232 | tf_op jit(solution)/shard_map/reduce_scatter | solution.py:97
  392.3 1.4 reshape.125
  394.6 1.0 convert_subtract_fusion
  (38 shorter events, 5.8 us)
Async XLA Ops:
  6.5 240.4 %copy-start = (bf16[128,128]{1,0:T(8,128)(2,1)S(1)}, bf16[128,128]{1,0:T(8,128)(2,1)}, u32[]{:S(2)}) copy-start(bf16[128,128]{1,0:T(8,128)(2,1)} %param.12) | copy-start | bytes 98308
  10.9 20.5 %all-to-all-start = ((s32[128,1,2]{2,1,0:T(1,128)}), s32[128,1,2]{2,1,0:T(1,128)S(1)}, u32[]{:S(2)}, u32[]{:S(2)}) async-start(s32[128,1,2]{2,1,0:T(1,128)} %bitcast.5), calls=%async_computation | async-start | bytes 131072 | tf_op jit(solution)/shard_map/all_to_all | solution.py:66
  31.3 21.0 %all-to-all-start.1 = ((bf16[128,2,1536]{2,1,0:T(2,128)(2,1)}), bf16[128,2,1536]{2,1,0:T(2,128)(2,1)S(1)}, u32[]{:S(2)}, u32[]{:S(2)}) async-start(bf16[128,2,1536]{2,1,0:T(2,128)(2,1)} %reshape.112), calls=%async_computation.1 | async-start | bytes 1572864 | tf_op jit(solution)/shard_map/all_to_all | solution.py:59
  57.7 5.0 %copy-start.2 = (s32[96,2]{0,1:T(2,128)S(1)}, s32[96,2]{0,1:T(2,128)}, u32[]{:S(2)}) copy-start(s32[96,2]{0,1:T(2,128)} %param.10) | copy-start | bytes 2308
  57.7 92.7 %all-to-all-start.2 = ((bf16[16,128,1536]{2,1,0:T(8,128)(2,1)}), bf16[16,128,1536]{2,1,0:T(8,128)(2,1)}, u32[]{:S(2)}, u32[]{:S(2)}) async-start(bf16[16,128,1536]{2,1,0:T(8,128)(2,1)} %stack.2), calls=%async_computation.2 | async-start | bytes 12582912 | tf_op jit(solution)/shard_map/all_to_all | solution.py:87
  62.5 182.7 %reduce-scatter.3.cloned.1.call-start = ((), (), s32[]{:S(2)}) async-start(), calls=%async_computation.5 | async-start | bytes 3538944 | tf_op jit(solution)/shard_map/reduce_scatter | solution.py:92
  162.0 150.4 %all-gather.2.cloned.1.call-start = ((), (), s32[]{:S(2)}) async-start(), calls=%async_computation.6 | async-start | bytes 3538944 | tf_op jit(solution)/shard_map/all_gather | solution.py:95
  250.6 141.7 %reduce-scatter.5.cloned.1.call-start = ((), (), s32[]{:S(2)}) async-start(), calls=%async_computation.7 | async-start | bytes 6684672 | tf_op jit(solution)/shard_map/reduce_scatter | solution.py:97
  323.7 70.4 %copy-start.1 = (bf16[128,128]{1,0:T(8,128)(2,1)S(1)}, bf16[128,128]{1,0:T(8,128)(2,1)}, u32[]{:S(2)}) copy-start(bf16[128,128]{1,0:T(8,128)(2,1)} %param.13) | copy-start | bytes 98308
Sparse Core Ops, SparseCore 0:
  162.1 83.0 reduce-scatter.2
  250.7 61.6 all-gather.1
  323.8 68.4 reduce-scatter.4
